TPU v7x, 256 devices: a whole 4x4x8 slice. The times are simulated.
256 devices in a mesh: req: 16 (over x_hi, y, core), ctx: 16 (over x_lo, z).
Axes of the slice: x: 4 (x_hi: 2, x_lo: 2; x = x_hi * 2 + x_lo), y: 4, z: 8, core: 2. Of those that a mesh axis runs over, the one named last changes fastest.
Arguments:
- queries: bfloat16 [1024, 8192], P(('req', 'ctx')), parts along dimension 0, may hold values from -15 to 15
- new_keys: bfloat16 [1024, 512], P(('req', 'ctx')), parts along dimension 0, may hold values from -9 to 9
- new_values: bfloat16 [1024, 512], P(('req', 'ctx')), parts along dimension 0, may hold values from -6 to 6
- cache_keys: bfloat16 [524288, 512], P(('req', 'ctx')), parts along dimension 0, may hold values from -6 to 6
- cache_values: bfloat16 [524288, 512], P(('req', 'ctx')), parts along dimension 0, may hold values from -6 to 6
- cache_length: int32 [16], P('req'), parts along dimension 0, may hold values from 8192 to 32767
- page_table: int32 [4096], P('req'), parts along dimension 0, may hold values from 0 to 255, each once
Outputs:
- attended: bfloat16 [1024, 8192], P(('req', 'ctx')), parts along dimension 0
There are 16 independent parts, one for each index of `req`. A program takes and returns all parts, laid end to end along the dimension named above; each array names one. Nothing has to cross between parts.
Inputs may be any that keep to these rules, and one draw needn't show every extreme that they name: A permutation: logical page p lies in physical rows page_table[p] * 128 to page_table[p] * 128 + 127.
All inputs are finite; a program needn't handle non-finite values.
Results may differ from a plain program's by a relative error of at most 0.004.
Values may be sent and summed in bfloat16 or wider, within the bound.
No kernel may reach another device: no remote copies, remote signals or barrier semaphores. Data moves between devices by JAX's collectives and lax.ppermute only.
A program may use at most 64 MiB of HBM per device.

v0:
```python
import jax
import jax.numpy as jnp
from jax import lax
from jax.sharding import PartitionSpec as P

KVH = 4
HD = 128
PAGE = 128
floor_score = -1e30


def from_behind(x, axis, by):
    devices = lax.axis_size(axis)
    return lax.ppermute(x, axis, [(i, (i + by) % devices) for i in range(devices)])


def attend(queries, query_pos, keys, values, key_pos, key_ok):
    rows = queries.shape[0]
    heads = queries.shape[1] // HD
    grouped = queries.reshape(rows, KVH, heads // KVH, HD)
    key_count = keys.shape[0]
    keys_grouped = keys.reshape(key_count, KVH, HD)
    values_grouped = values.reshape(key_count, KVH, HD)
    scores = jnp.einsum(
        "rkgd,nkd->rkgn", grouped, keys_grouped, preferred_element_type=jnp.float32
    ) * HD ** (-0.5)
    allowed = key_ok[None, :] & (key_pos[None, :] <= query_pos[:, None])
    allowed = allowed[:, None, None, :]
    scores = jnp.where(allowed, scores, floor_score)
    top = jnp.max(scores, axis=3)
    weights = jnp.where(allowed, jnp.exp(scores - top[..., None]), 0.0)
    total = jnp.sum(weights, axis=3)
    mixed = jnp.einsum(
        "rkgn,nkd->rkgd",
        weights.astype(jnp.bfloat16),
        values_grouped,
        preferred_element_type=jnp.float32,
    )
    return (mixed.reshape(rows, heads * HD), top.reshape(rows, heads), total.reshape(rows, heads))


def combine(first, second):
    mixed_first, top_first, total_first = first
    mixed_second, top_second, total_second = second
    rows, heads = top_first.shape
    top = jnp.maximum(top_first, top_second)
    factor_first = jnp.exp(top_first - top)
    factor_second = jnp.exp(top_second - top)
    mixed = (
        mixed_first.reshape(rows, heads, HD) * factor_first[..., None]
        + mixed_second.reshape(rows, heads, HD) * factor_second[..., None]
    )
    return (
        mixed.reshape(rows, heads * HD),
        top,
        factor_first * total_first + factor_second * total_second,
    )


def empty_state(rows, heads):
    return (
        jnp.zeros((rows, heads * HD), jnp.float32),
        jnp.full((rows, heads), floor_score, jnp.float32),
        jnp.zeros((rows, heads), jnp.float32),
    )


def settle(moved):
    return (moved[0], moved[1], moved[2], moved[3])


def local(queries, new_keys, new_values, cache_keys, cache_values, cache_length, page_table):
    count = lax.axis_size("ctx")
    device = lax.axis_index("ctx")
    rows = queries.shape[0]
    heads = queries.shape[1] // HD
    local_pages = cache_keys.shape[0] // PAGE
    length = cache_length[0]
    slots = device * local_pages + lax.iota(jnp.int32, local_pages)
    hits = (page_table[:, None] == slots[None, :]).astype(jnp.int32)
    logical = jnp.sum(hits * lax.iota(jnp.int32, page_table.shape[0])[:, None], axis=0)
    cache_pos = (logical[:, None] * PAGE + lax.iota(jnp.int32, PAGE)[None, :]).reshape(-1)
    cache_live = cache_pos < length
    own_pos = length + device * rows + lax.iota(jnp.int32, rows)

    def attend_cache(held, positions):
        return attend(held, positions, cache_keys, cache_values, cache_pos, cache_live)

    keys_piece = lax.all_gather(new_keys, "ctx", axis=0, tiled=True)
    values_piece = lax.all_gather(new_values, "ctx", axis=0, tiled=True)
    piece_rows = keys_piece.shape[0]
    key_pos = length + lax.iota(jnp.int32, piece_rows)
    span_state = combine(
        empty_state(rows, heads),
        attend(queries, own_pos, keys_piece, values_piece, key_pos, jnp.ones((piece_rows,), bool)),
    )

    def hop_one(step, carry):
        held = carry[0]
        source = (device - step) % count
        positions = length + source * rows + lax.iota(jnp.int32, rows)
        state = combine(carry[1:4], attend_cache(held, positions))
        return settle(from_behind((held,) + state, "ctx", 1))

    final = lax.fori_loop(0, count, hop_one, (queries,) + empty_state(rows, heads))
    cycle_state = final[1:4]
    mixed, top, total = combine(cycle_state, span_state)
    result = mixed.reshape(rows, heads, HD) / total[..., None]
    return result.reshape(rows, heads * HD).astype(jnp.bfloat16)


def solution(mesh):
    in_specs = (
        P(("req", "ctx"), None),
        P(("req", "ctx"), None),
        P(("req", "ctx"), None),
        P(("req", "ctx"), None),
        P(("req", "ctx"), None),
        P("req"),
        P("req"),
    )
    out_specs = P(("req", "ctx"), None)
    return jax.shard_map(local, mesh=mesh, in_specs=in_specs, out_specs=out_specs, check_vma=False)
```

profile of v0, /device:TPU:2, one launch (start us, length us, event | category | flops | bytes accessed | tf_op | source)
XLA Modules:
  0.0 324.2 jit_solution(2116719299812118511)
XLA Ops:
  2.5 35.9 %all-gather = bf16[16,4,512]{2,1,0:T(4,128)(2,1)S(1)} all-gather(bf16[1,4,512]{2,1,0:T(4,128)(2,1)} %bitcast.139), channel_id=1, replica_groups=mesh['req'=16,'ctx'=16] {'ctx'}, dimensions={0}, use_global_device_ids=true | all-gather | bytes 69632 | tf_op jit(solution)/shard_map/all_gather | solution.py:89
  38.4 30.2 %all-gather.1 = bf16[16,4,512]{2,1,0:T(4,128)(2,1)S(1)} all-gather(bf16[1,4,512]{2,1,0:T(4,128)(2,1)} %bitcast.140), channel_id=1, replica_groups=mesh['req'=16,'ctx'=16] {'ctx'}, dimensions={0}, use_global_device_ids=true | all-gather | bytes 69632 | tf_op jit(solution)/shard_map/all_gather | solution.py:90
  69.5 4.1 %reshape.248 = bf16[2048,4,128]{2,1,0:T(4,128)(2,1)} reshape(bf16[2048,512]{1,0:T(8,128)(2,1)} %param.12) | data formatting | bytes 4194304 | tf_op jit(solution)/shard_map/while/body/eval_jaxpr/reshape | solution.py:22
  75.7 247.0 %while.24 = (s32[]{:T(128)}, bf16[4,8192]{1,0:T(4,128)(2,1)S(1)}, f32[4,8192]{1,0:T(4,128)S(1)}, f32[4,64]{1,0:T(4,128)S(1)}, f32[4,64]{1,0:T(4,128)S(1)}, /*ind...) while((s32[]{:T(128)}, bf16[4,8192]{1,0:T(4,128)(2,1)S(1)}, ...), condition=%wide.wide.region_4.5_spmd.clone.clone, body=%wide.wide.region_1.4_spmd.clone.clone.sunk | while | flops 273275904 | bytes 21383824 | solution.py:105
  77.4 2.5 fusion.68
  85.1 6.5 %collective-permute-done.2 = f32[4,64]{1,0:T(4,128)S(1)} collective-permute-done((f32[4,64]{1,0:T(4,128)S(1)}, f32[4,64]{1,0:T(4,128)S(1)}, u32[]{:S(2)}, u32[]{:S(2)}) %collective-permute-start.2) | collective-permute-done | bytes 1056 | tf_op jit(solution)/shard_map/while/body/eval_jaxpr/ppermute | solution.py:14
  93.3 2.5 fusion.68
  99.5 3.5 %collective-permute-start.3 = (f32[4,64]{1,0:T(4,128)S(1)}, f32[4,64]{1,0:T(4,128)S(1)}, u32[]{:S(2)}, u32[]{:S(2)}) collective-permute-start(f32[4,64]{1,0:T(4,128)S(1)} %get-tuple-element.509), channel_id=1, source_target_pairs={{0,1},{1,2},{2,3},{3,4},{4,5},{5,6},{6,7},{7,8},{8,9},{9,10},{10,1... | collective-permute-start | bytes 3080 | tf_op jit(solution)/shard_map/while/body/eval_jaxpr/ppermute | solution.py:14
  103.0 3.8 %collective-permute-done.2 = f32[4,64]{1,0:T(4,128)S(1)} collective-permute-done((f32[4,64]{1,0:T(4,128)S(1)}, f32[4,64]{1,0:T(4,128)S(1)}, u32[]{:S(2)}, u32[]{:S(2)}) %collective-permute-start.2) | collective-permute-done | bytes 1056 | tf_op jit(solution)/shard_map/while/body/eval_jaxpr/ppermute | solution.py:14
  108.4 2.5 fusion.68
  118.0 3.8 %collective-permute-done.2 = f32[4,64]{1,0:T(4,128)S(1)} collective-permute-done((f32[4,64]{1,0:T(4,128)S(1)}, f32[4,64]{1,0:T(4,128)S(1)}, u32[]{:S(2)}, u32[]{:S(2)}) %collective-permute-start.2) | collective-permute-done | bytes 1056 | tf_op jit(solution)/shard_map/while/body/eval_jaxpr/ppermute | solution.py:14
  124.0 2.5 fusion.68
  132.8 4.6 %collective-permute-done.2 = f32[4,64]{1,0:T(4,128)S(1)} collective-permute-done((f32[4,64]{1,0:T(4,128)S(1)}, f32[4,64]{1,0:T(4,128)S(1)}, u32[]{:S(2)}, u32[]{:S(2)}) %collective-permute-start.2) | collective-permute-done | bytes 1056 | tf_op jit(solution)/shard_map/while/body/eval_jaxpr/ppermute | solution.py:14
  139.0 2.5 fusion.68
  147.8 4.6 %collective-permute-done.2 = f32[4,64]{1,0:T(4,128)S(1)} collective-permute-done((f32[4,64]{1,0:T(4,128)S(1)}, f32[4,64]{1,0:T(4,128)S(1)}, u32[]{:S(2)}, u32[]{:S(2)}) %collective-permute-start.2) | collective-permute-done | bytes 1056 | tf_op jit(solution)/shard_map/while/body/eval_jaxpr/ppermute | solution.py:14
  154.1 2.5 fusion.68
  162.9 4.6 %collective-permute-done.2 = f32[4,64]{1,0:T(4,128)S(1)} collective-permute-done((f32[4,64]{1,0:T(4,128)S(1)}, f32[4,64]{1,0:T(4,128)S(1)}, u32[]{:S(2)}, u32[]{:S(2)}) %collective-permute-start.2) | collective-permute-done | bytes 1056 | tf_op jit(solution)/shard_map/while/body/eval_jaxpr/ppermute | solution.py:14
  169.1 2.5 fusion.68
  177.9 4.6 %collective-permute-done.2 = f32[4,64]{1,0:T(4,128)S(1)} collective-permute-done((f32[4,64]{1,0:T(4,128)S(1)}, f32[4,64]{1,0:T(4,128)S(1)}, u32[]{:S(2)}, u32[]{:S(2)}) %collective-permute-start.2) | collective-permute-done | bytes 1056 | tf_op jit(solution)/shard_map/while/body/eval_jaxpr/ppermute | solution.py:14
  184.2 2.5 fusion.68
  193.5 4.1 %collective-permute-done.2 = f32[4,64]{1,0:T(4,128)S(1)} collective-permute-done((f32[4,64]{1,0:T(4,128)S(1)}, f32[4,64]{1,0:T(4,128)S(1)}, u32[]{:S(2)}, u32[]{:S(2)}) %collective-permute-start.2) | collective-permute-done | bytes 1056 | tf_op jit(solution)/shard_map/while/body/eval_jaxpr/ppermute | solution.py:14
  208.5 4.1 %collective-permute-done.2 = f32[4,64]{1,0:T(4,128)S(1)} collective-permute-done((f32[4,64]{1,0:T(4,128)S(1)}, f32[4,64]{1,0:T(4,128)S(1)}, u32[]{:S(2)}, u32[]{:S(2)}) %collective-permute-start.2) | collective-permute-done | bytes 1056 | tf_op jit(solution)/shard_map/while/body/eval_jaxpr/ppermute | solution.py:14
  223.6 4.0 %collective-permute-done.2 = f32[4,64]{1,0:T(4,128)S(1)} collective-permute-done((f32[4,64]{1,0:T(4,128)S(1)}, f32[4,64]{1,0:T(4,128)S(1)}, u32[]{:S(2)}, u32[]{:S(2)}) %collective-permute-start.2) | collective-permute-done | bytes 1056 | tf_op jit(solution)/shard_map/while/body/eval_jaxpr/ppermute | solution.py:14
  236.2 2.5 collective-permute-start.3
  238.8 4.9 %collective-permute-done.2 = f32[4,64]{1,0:T(4,128)S(1)} collective-permute-done((f32[4,64]{1,0:T(4,128)S(1)}, f32[4,64]{1,0:T(4,128)S(1)}, u32[]{:S(2)}, u32[]{:S(2)}) %collective-permute-start.2) | collective-permute-done | bytes 1056 | tf_op jit(solution)/shard_map/while/body/eval_jaxpr/ppermute | solution.py:14
  251.3 3.3 %collective-permute-start.3 = (f32[4,64]{1,0:T(4,128)S(1)}, f32[4,64]{1,0:T(4,128)S(1)}, u32[]{:S(2)}, u32[]{:S(2)}) collective-permute-start(f32[4,64]{1,0:T(4,128)S(1)} %get-tuple-element.509), channel_id=1, source_target_pairs={{0,1},{1,2},{2,3},{3,4},{4,5},{5,6},{6,7},{7,8},{8,9},{9,10},{10,1... | collective-permute-start | bytes 3080 | tf_op jit(solution)/shard_map/while/body/eval_jaxpr/ppermute | solution.py:14
  254.6 6.2 %collective-permute-done.2 = f32[4,64]{1,0:T(4,128)S(1)} collective-permute-done((f32[4,64]{1,0:T(4,128)S(1)}, f32[4,64]{1,0:T(4,128)S(1)}, u32[]{:S(2)}, u32[]{:S(2)}) %collective-permute-start.2) | collective-permute-done | bytes 1056 | tf_op jit(solution)/shard_map/while/body/eval_jaxpr/ppermute | solution.py:14
  270.2 7.0 %collective-permute-done.2 = f32[4,64]{1,0:T(4,128)S(1)} collective-permute-done((f32[4,64]{1,0:T(4,128)S(1)}, f32[4,64]{1,0:T(4,128)S(1)}, u32[]{:S(2)}, u32[]{:S(2)}) %collective-permute-start.2) | collective-permute-done | bytes 1056 | tf_op jit(solution)/shard_map/while/body/eval_jaxpr/ppermute | solution.py:14
  278.8 2.5 fusion.68
  285.2 7.5 %collective-permute-done.2 = f32[4,64]{1,0:T(4,128)S(1)} collective-permute-done((f32[4,64]{1,0:T(4,128)S(1)}, f32[4,64]{1,0:T(4,128)S(1)}, u32[]{:S(2)}, u32[]{:S(2)}) %collective-permute-start.2) | collective-permute-done | bytes 1056 | tf_op jit(solution)/shard_map/while/body/eval_jaxpr/ppermute | solution.py:14
  301.8 5.9 %collective-permute-done.2 = f32[4,64]{1,0:T(4,128)S(1)} collective-permute-done((f32[4,64]{1,0:T(4,128)S(1)}, f32[4,64]{1,0:T(4,128)S(1)}, u32[]{:S(2)}, u32[]{:S(2)}) %collective-permute-start.2) | collective-permute-done | bytes 1056 | tf_op jit(solution)/shard_map/while/body/eval_jaxpr/ppermute | solution.py:14
  317.6 5.2 %collective-permute-done.2 = f32[4,64]{1,0:T(4,128)S(1)} collective-permute-done((f32[4,64]{1,0:T(4,128)S(1)}, f32[4,64]{1,0:T(4,128)S(1)}, u32[]{:S(2)}, u32[]{:S(2)}) %collective-permute-start.2) | collective-permute-done | bytes 1056 | tf_op jit(solution)/shard_map/while/body/eval_jaxpr/ppermute | solution.py:14
  (433 shorter events, 127.5 us)
Async XLA Ops:
  82.9 8.8 %collective-permute-start.1 = (f32[4,8192]{1,0:T(4,128)S(1)}, f32[4,8192]{1,0:T(4,128)S(1)}, u32[]{:S(2)}, u32[]{:S(2)}) collective-permute-start(f32[4,8192]{1,0:T(4,128)S(1)} %fusion.71), channel_id=1, source_target_pairs={{0,1},{1,2},{2,3},{3,4},{4,5},{5,6},{6,7},{7,8},{8,9},{9,10},{10,1... | collective-permute-start | bytes 393224 | tf_op jit(solution)/shard_map/while/body/eval_jaxpr/ppermute | solution.py:14
  98.9 8.0 %collective-permute-start.1 = (f32[4,8192]{1,0:T(4,128)S(1)}, f32[4,8192]{1,0:T(4,128)S(1)}, u32[]{:S(2)}, u32[]{:S(2)}) collective-permute-start(f32[4,8192]{1,0:T(4,128)S(1)} %fusion.71), channel_id=1, source_target_pairs={{0,1},{1,2},{2,3},{3,4},{4,5},{5,6},{6,7},{7,8},{8,9},{9,10},{10,1... | collective-permute-start | bytes 393224 | tf_op jit(solution)/shard_map/while/body/eval_jaxpr/ppermute | solution.py:14
  98.9 7.9 %collective-permute-start = (bf16[4,8192]{1,0:T(4,128)(2,1)S(1)}, bf16[4,8192]{1,0:T(4,128)(2,1)S(1)}, u32[]{:S(2)}, u32[]{:S(2)}) collective-permute-start(bf16[4,8192]{1,0:T(4,128)(2,1)S(1)} %copy.160), channel_id=1, source_target_pairs={{0,1},{1,2},{2,3},{3,4},{4,5},{5,6},{6,7},{7,8},{8,9},{9,10},{10,1... | collective-permute-start | bytes 196616 | tf_op jit(solution)/shard_map/while/body/eval_jaxpr/ppermute | solution.py:14
  113.9 8.5 %collective-permute-start.1 = (f32[4,8192]{1,0:T(4,128)S(1)}, f32[4,8192]{1,0:T(4,128)S(1)}, u32[]{:S(2)}, u32[]{:S(2)}) collective-permute-start(f32[4,8192]{1,0:T(4,128)S(1)} %fusion.71), channel_id=1, source_target_pairs={{0,1},{1,2},{2,3},{3,4},{4,5},{5,6},{6,7},{7,8},{8,9},{9,10},{10,1... | collective-permute-start | bytes 393224 | tf_op jit(solution)/shard_map/while/body/eval_jaxpr/ppermute | solution.py:14
  114.0 8.4 %collective-permute-start = (bf16[4,8192]{1,0:T(4,128)(2,1)S(1)}, bf16[4,8192]{1,0:T(4,128)(2,1)S(1)}, u32[]{:S(2)}, u32[]{:S(2)}) collective-permute-start(bf16[4,8192]{1,0:T(4,128)(2,1)S(1)} %copy.160), channel_id=1, source_target_pairs={{0,1},{1,2},{2,3},{3,4},{4,5},{5,6},{6,7},{7,8},{8,9},{9,10},{10,1... | collective-permute-start | bytes 196616 | tf_op jit(solution)/shard_map/while/body/eval_jaxpr/ppermute | solution.py:14
  129.5 7.9 %collective-permute-start.1 = (f32[4,8192]{1,0:T(4,128)S(1)}, f32[4,8192]{1,0:T(4,128)S(1)}, u32[]{:S(2)}, u32[]{:S(2)}) collective-permute-start(f32[4,8192]{1,0:T(4,128)S(1)} %fusion.71), channel_id=1, source_target_pairs={{0,1},{1,2},{2,3},{3,4},{4,5},{5,6},{6,7},{7,8},{8,9},{9,10},{10,1... | collective-permute-start | bytes 393224 | tf_op jit(solution)/shard_map/while/body/eval_jaxpr/ppermute | solution.py:14
  129.6 7.8 %collective-permute-start = (bf16[4,8192]{1,0:T(4,128)(2,1)S(1)}, bf16[4,8192]{1,0:T(4,128)(2,1)S(1)}, u32[]{:S(2)}, u32[]{:S(2)}) collective-permute-start(bf16[4,8192]{1,0:T(4,128)(2,1)S(1)} %copy.160), channel_id=1, source_target_pairs={{0,1},{1,2},{2,3},{3,4},{4,5},{5,6},{6,7},{7,8},{8,9},{9,10},{10,1... | collective-permute-start | bytes 196616 | tf_op jit(solution)/shard_map/while/body/eval_jaxpr/ppermute | solution.py:14
  144.6 7.9 %collective-permute-start.1 = (f32[4,8192]{1,0:T(4,128)S(1)}, f32[4,8192]{1,0:T(4,128)S(1)}, u32[]{:S(2)}, u32[]{:S(2)}) collective-permute-start(f32[4,8192]{1,0:T(4,128)S(1)} %fusion.71), channel_id=1, source_target_pairs={{0,1},{1,2},{2,3},{3,4},{4,5},{5,6},{6,7},{7,8},{8,9},{9,10},{10,1... | collective-permute-start | bytes 393224 | tf_op jit(solution)/shard_map/while/body/eval_jaxpr/ppermute | solution.py:14
  144.7 7.8 %collective-permute-start = (bf16[4,8192]{1,0:T(4,128)(2,1)S(1)}, bf16[4,8192]{1,0:T(4,128)(2,1)S(1)}, u32[]{:S(2)}, u32[]{:S(2)}) collective-permute-start(bf16[4,8192]{1,0:T(4,128)(2,1)S(1)} %copy.160), channel_id=1, source_target_pairs={{0,1},{1,2},{2,3},{3,4},{4,5},{5,6},{6,7},{7,8},{8,9},{9,10},{10,1... | collective-permute-start | bytes 196616 | tf_op jit(solution)/shard_map/while/body/eval_jaxpr/ppermute | solution.py:14
  159.6 7.9 %collective-permute-start.1 = (f32[4,8192]{1,0:T(4,128)S(1)}, f32[4,8192]{1,0:T(4,128)S(1)}, u32[]{:S(2)}, u32[]{:S(2)}) collective-permute-start(f32[4,8192]{1,0:T(4,128)S(1)} %fusion.71), channel_id=1, source_target_pairs={{0,1},{1,2},{2,3},{3,4},{4,5},{5,6},{6,7},{7,8},{8,9},{9,10},{10,1... | collective-permute-start | bytes 393224 | tf_op jit(solution)/shard_map/while/body/eval_jaxpr/ppermute | solution.py:14
  159.7 7.8 %collective-permute-start = (bf16[4,8192]{1,0:T(4,128)(2,1)S(1)}, bf16[4,8192]{1,0:T(4,128)(2,1)S(1)}, u32[]{:S(2)}, u32[]{:S(2)}) collective-permute-start(bf16[4,8192]{1,0:T(4,128)(2,1)S(1)} %copy.160), channel_id=1, source_target_pairs={{0,1},{1,2},{2,3},{3,4},{4,5},{5,6},{6,7},{7,8},{8,9},{9,10},{10,1... | collective-permute-start | bytes 196616 | tf_op jit(solution)/shard_map/while/body/eval_jaxpr/ppermute | solution.py:14
  174.6 7.9 %collective-permute-start.1 = (f32[4,8192]{1,0:T(4,128)S(1)}, f32[4,8192]{1,0:T(4,128)S(1)}, u32[]{:S(2)}, u32[]{:S(2)}) collective-permute-start(f32[4,8192]{1,0:T(4,128)S(1)} %fusion.71), channel_id=1, source_target_pairs={{0,1},{1,2},{2,3},{3,4},{4,5},{5,6},{6,7},{7,8},{8,9},{9,10},{10,1... | collective-permute-start | bytes 393224 | tf_op jit(solution)/shard_map/while/body/eval_jaxpr/ppermute | solution.py:14
  189.7 7.9 %collective-permute-start.1 = (f32[4,8192]{1,0:T(4,128)S(1)}, f32[4,8192]{1,0:T(4,128)S(1)}, u32[]{:S(2)}, u32[]{:S(2)}) collective-permute-start(f32[4,8192]{1,0:T(4,128)S(1)} %fusion.71), channel_id=1, source_target_pairs={{0,1},{1,2},{2,3},{3,4},{4,5},{5,6},{6,7},{7,8},{8,9},{9,10},{10,1... | collective-permute-start | bytes 393224 | tf_op jit(solution)/shard_map/while/body/eval_jaxpr/ppermute | solution.py:14
  204.7 7.9 %collective-permute-start.1 = (f32[4,8192]{1,0:T(4,128)S(1)}, f32[4,8192]{1,0:T(4,128)S(1)}, u32[]{:S(2)}, u32[]{:S(2)}) collective-permute-start(f32[4,8192]{1,0:T(4,128)S(1)} %fusion.71), channel_id=1, source_target_pairs={{0,1},{1,2},{2,3},{3,4},{4,5},{5,6},{6,7},{7,8},{8,9},{9,10},{10,1... | collective-permute-start | bytes 393224 | tf_op jit(solution)/shard_map/while/body/eval_jaxpr/ppermute | solution.py:14
  219.8 7.9 %collective-permute-start.1 = (f32[4,8192]{1,0:T(4,128)S(1)}, f32[4,8192]{1,0:T(4,128)S(1)}, u32[]{:S(2)}, u32[]{:S(2)}) collective-permute-start(f32[4,8192]{1,0:T(4,128)S(1)} %fusion.71), channel_id=1, source_target_pairs={{0,1},{1,2},{2,3},{3,4},{4,5},{5,6},{6,7},{7,8},{8,9},{9,10},{10,1... | collective-permute-start | bytes 393224 | tf_op jit(solution)/shard_map/while/body/eval_jaxpr/ppermute | solution.py:14
  234.8 8.9 %collective-permute-start.1 = (f32[4,8192]{1,0:T(4,128)S(1)}, f32[4,8192]{1,0:T(4,128)S(1)}, u32[]{:S(2)}, u32[]{:S(2)}) collective-permute-start(f32[4,8192]{1,0:T(4,128)S(1)} %fusion.71), channel_id=1, source_target_pairs={{0,1},{1,2},{2,3},{3,4},{4,5},{5,6},{6,7},{7,8},{8,9},{9,10},{10,1... | collective-permute-start | bytes 393224 | tf_op jit(solution)/shard_map/while/body/eval_jaxpr/ppermute | solution.py:14
  234.9 8.8 %collective-permute-start = (bf16[4,8192]{1,0:T(4,128)(2,1)S(1)}, bf16[4,8192]{1,0:T(4,128)(2,1)S(1)}, u32[]{:S(2)}, u32[]{:S(2)}) collective-permute-start(bf16[4,8192]{1,0:T(4,128)(2,1)S(1)} %copy.160), channel_id=1, source_target_pairs={{0,1},{1,2},{2,3},{3,4},{4,5},{5,6},{6,7},{7,8},{8,9},{9,10},{10,1... | collective-permute-start | bytes 196616 | tf_op jit(solution)/shard_map/while/body/eval_jaxpr/ppermute | solution.py:14
  250.8 10.0 %collective-permute-start.1 = (f32[4,8192]{1,0:T(4,128)S(1)}, f32[4,8192]{1,0:T(4,128)S(1)}, u32[]{:S(2)}, u32[]{:S(2)}) collective-permute-start(f32[4,8192]{1,0:T(4,128)S(1)} %fusion.71), channel_id=1, source_target_pairs={{0,1},{1,2},{2,3},{3,4},{4,5},{5,6},{6,7},{7,8},{8,9},{9,10},{10,1... | collective-permute-start | bytes 393224 | tf_op jit(solution)/shard_map/while/body/eval_jaxpr/ppermute | solution.py:14
  250.9 9.9 %collective-permute-start = (bf16[4,8192]{1,0:T(4,128)(2,1)S(1)}, bf16[4,8192]{1,0:T(4,128)(2,1)S(1)}, u32[]{:S(2)}, u32[]{:S(2)}) collective-permute-start(bf16[4,8192]{1,0:T(4,128)(2,1)S(1)} %copy.160), channel_id=1, source_target_pairs={{0,1},{1,2},{2,3},{3,4},{4,5},{5,6},{6,7},{7,8},{8,9},{9,10},{10,1... | collective-permute-start | bytes 196616 | tf_op jit(solution)/shard_map/while/body/eval_jaxpr/ppermute | solution.py:14
  251.2 9.6 %collective-permute-start.2 = (f32[4,64]{1,0:T(4,128)S(1)}, f32[4,64]{1,0:T(4,128)S(1)}, u32[]{:S(2)}, u32[]{:S(2)}) collective-permute-start(f32[4,64]{1,0:T(4,128)S(1)} %get-tuple-element.508), channel_id=1, source_target_pairs={{0,1},{1,2},{2,3},{3,4},{4,5},{5,6},{6,7},{7,8},{8,9},{9,10},{10,1... | collective-permute-start | bytes 3080 | tf_op jit(solution)/shard_map/while/body/eval_jaxpr/ppermute | solution.py:14
  251.3 9.6 %collective-permute-start.3 = (f32[4,64]{1,0:T(4,128)S(1)}, f32[4,64]{1,0:T(4,128)S(1)}, u32[]{:S(2)}, u32[]{:S(2)}) collective-permute-start(f32[4,64]{1,0:T(4,128)S(1)} %get-tuple-element.509), channel_id=1, source_target_pairs={{0,1},{1,2},{2,3},{3,4},{4,5},{5,6},{6,7},{7,8},{8,9},{9,10},{10,1... | collective-permute-start | bytes 3080 | tf_op jit(solution)/shard_map/while/body/eval_jaxpr/ppermute | solution.py:14
  268.0 9.2 %collective-permute-start.1 = (f32[4,8192]{1,0:T(4,128)S(1)}, f32[4,8192]{1,0:T(4,128)S(1)}, u32[]{:S(2)}, u32[]{:S(2)}) collective-permute-start(f32[4,8192]{1,0:T(4,128)S(1)} %fusion.71), channel_id=1, source_target_pairs={{0,1},{1,2},{2,3},{3,4},{4,5},{5,6},{6,7},{7,8},{8,9},{9,10},{10,1... | collective-permute-start | bytes 393224 | tf_op jit(solution)/shard_map/while/body/eval_jaxpr/ppermute | solution.py:14
  268.1 9.1 %collective-permute-start = (bf16[4,8192]{1,0:T(4,128)(2,1)S(1)}, bf16[4,8192]{1,0:T(4,128)(2,1)S(1)}, u32[]{:S(2)}, u32[]{:S(2)}) collective-permute-start(bf16[4,8192]{1,0:T(4,128)(2,1)S(1)} %copy.160), channel_id=1, source_target_pairs={{0,1},{1,2},{2,3},{3,4},{4,5},{5,6},{6,7},{7,8},{8,9},{9,10},{10,1... | collective-permute-start | bytes 196616 | tf_op jit(solution)/shard_map/while/body/eval_jaxpr/ppermute | solution.py:14
  268.1 9.0 %collective-permute-start.2 = (f32[4,64]{1,0:T(4,128)S(1)}, f32[4,64]{1,0:T(4,128)S(1)}, u32[]{:S(2)}, u32[]{:S(2)}) collective-permute-start(f32[4,64]{1,0:T(4,128)S(1)} %get-tuple-element.508), channel_id=1, source_target_pairs={{0,1},{1,2},{2,3},{3,4},{4,5},{5,6},{6,7},{7,8},{8,9},{9,10},{10,1... | collective-permute-start | bytes 3080 | tf_op jit(solution)/shard_map/while/body/eval_jaxpr/ppermute | solution.py:14
  268.2 9.0 %collective-permute-start.3 = (f32[4,64]{1,0:T(4,128)S(1)}, f32[4,64]{1,0:T(4,128)S(1)}, u32[]{:S(2)}, u32[]{:S(2)}) collective-permute-start(f32[4,64]{1,0:T(4,128)S(1)} %get-tuple-element.509), channel_id=1, source_target_pairs={{0,1},{1,2},{2,3},{3,4},{4,5},{5,6},{6,7},{7,8},{8,9},{9,10},{10,1... | collective-permute-start | bytes 3080 | tf_op jit(solution)/shard_map/while/body/eval_jaxpr/ppermute | solution.py:14
  284.3 8.4 %collective-permute-start.1 = (f32[4,8192]{1,0:T(4,128)S(1)}, f32[4,8192]{1,0:T(4,128)S(1)}, u32[]{:S(2)}, u32[]{:S(2)}) collective-permute-start(f32[4,8192]{1,0:T(4,128)S(1)} %fusion.71), channel_id=1, source_target_pairs={{0,1},{1,2},{2,3},{3,4},{4,5},{5,6},{6,7},{7,8},{8,9},{9,10},{10,1... | collective-permute-start | bytes 393224 | tf_op jit(solution)/shard_map/while/body/eval_jaxpr/ppermute | solution.py:14
  284.4 8.3 %collective-permute-start = (bf16[4,8192]{1,0:T(4,128)(2,1)S(1)}, bf16[4,8192]{1,0:T(4,128)(2,1)S(1)}, u32[]{:S(2)}, u32[]{:S(2)}) collective-permute-start(bf16[4,8192]{1,0:T(4,128)(2,1)S(1)} %copy.160), channel_id=1, source_target_pairs={{0,1},{1,2},{2,3},{3,4},{4,5},{5,6},{6,7},{7,8},{8,9},{9,10},{10,1... | collective-permute-start | bytes 196616 | tf_op jit(solution)/shard_map/while/body/eval_jaxpr/ppermute | solution.py:14
  284.5 8.2 %collective-permute-start.2 = (f32[4,64]{1,0:T(4,128)S(1)}, f32[4,64]{1,0:T(4,128)S(1)}, u32[]{:S(2)}, u32[]{:S(2)}) collective-permute-start(f32[4,64]{1,0:T(4,128)S(1)} %get-tuple-element.508), channel_id=1, source_target_pairs={{0,1},{1,2},{2,3},{3,4},{4,5},{5,6},{6,7},{7,8},{8,9},{9,10},{10,1... | collective-permute-start | bytes 3080 | tf_op jit(solution)/shard_map/while/body/eval_jaxpr/ppermute | solution.py:14
  284.6 8.1 %collective-permute-start.3 = (f32[4,64]{1,0:T(4,128)S(1)}, f32[4,64]{1,0:T(4,128)S(1)}, u32[]{:S(2)}, u32[]{:S(2)}) collective-permute-start(f32[4,64]{1,0:T(4,128)S(1)} %get-tuple-element.509), channel_id=1, source_target_pairs={{0,1},{1,2},{2,3},{3,4},{4,5},{5,6},{6,7},{7,8},{8,9},{9,10},{10,1... | collective-permute-start | bytes 3080 | tf_op jit(solution)/shard_map/while/body/eval_jaxpr/ppermute | solution.py:14
  299.8 7.9 %collective-permute-start.1 = (f32[4,8192]{1,0:T(4,128)S(1)}, f32[4,8192]{1,0:T(4,128)S(1)}, u32[]{:S(2)}, u32[]{:S(2)}) collective-permute-start(f32[4,8192]{1,0:T(4,128)S(1)} %fusion.71), channel_id=1, source_target_pairs={{0,1},{1,2},{2,3},{3,4},{4,5},{5,6},{6,7},{7,8},{8,9},{9,10},{10,1... | collective-permute-start | bytes 393224 | tf_op jit(solution)/shard_map/while/body/eval_jaxpr/ppermute | solution.py:14
  314.9 7.9 %collective-permute-start.1 = (f32[4,8192]{1,0:T(4,128)S(1)}, f32[4,8192]{1,0:T(4,128)S(1)}, u32[]{:S(2)}, u32[]{:S(2)}) collective-permute-start(f32[4,8192]{1,0:T(4,128)S(1)} %fusion.71), channel_id=1, source_target_pairs={{0,1},{1,2},{2,3},{3,4},{4,5},{5,6},{6,7},{7,8},{8,9},{9,10},{10,1... | collective-permute-start | bytes 393224 | tf_op jit(solution)/shard_map/while/body/eval_jaxpr/ppermute | solution.py:14
  315.0 7.8 %collective-permute-start = (bf16[4,8192]{1,0:T(4,128)(2,1)S(1)}, bf16[4,8192]{1,0:T(4,128)(2,1)S(1)}, u32[]{:S(2)}, u32[]{:S(2)}) collective-permute-start(bf16[4,8192]{1,0:T(4,128)(2,1)S(1)} %copy.160), channel_id=1, source_target_pairs={{0,1},{1,2},{2,3},{3,4},{4,5},{5,6},{6,7},{7,8},{8,9},{9,10},{10,1... | collective-permute-start | bytes 196616 | tf_op jit(solution)/shard_map/while/body/eval_jaxpr/ppermute | solution.py:14
  (49 other events, 254.3 us)
where the time goes:
time: 326 us; the launch traced here: 324 us
  waiting for transfers between devices  82.5 us (25%)
  blocking collectives  66.1 us (20%)
  matrix products  53.6 us (16%)
  starting transfers between devices  50.2 us (15%)
  local copies, waits for them, and re-layouts  29.6 us (9%)
  other arithmetic  29.3 us (9%)
  loops' own time  12.3 us (4%)
    ppermute x64, waiting for transfers between devices, from_behind(): lax.ppermute(x, axis, [(i, (i + by) % devices) for i in range(devices)])  82.5 us
    ppermute x64, starting transfers between devices, from_behind(): lax.ppermute(x, axis, [(i, (i + by) % devices) for i in range(devices)])  50.2 us
    dot_general x17, matrix products, attend(): jnp.einsum('rkgd,nkd->rkgn', grouped, keys_grouped, preferred_element_typ...  40.8 us
    all_gather x1, blocking collectives, local(): keys_piece = lax.all_gather(new_keys, 'ctx', axis=0, tiled=True)  35.9 us
    all_gather x1, blocking collectives, local(): values_piece = lax.all_gather(new_values, 'ctx', axis=0, tiled=True)  30.2 us
    while x80, local copies, waits for them, and re-layouts  19 us
    dot_general x17, matrix products, attend(): jnp.einsum('rkgn,nkd->rkgd', weights.astype(jnp.bfloat16), values_grouped...  12.8 us
    another operation x1, loops' own time, local(): lax.fori_loop(0, count, hop_one, (queries,) + empty_state(rows, heads))  12.3 us
  transfers between devices with their start and end apart: 64, of which 17 were waited for; matrix products, arithmetic and copies ran while one was open for 0% of the time, Pallas kernels for 0%

commit v1 on v0

--- a/solution.py
+++ b/solution.py
@@ -87,7 +87,9 @@
         return attend(held, positions, cache_keys, cache_values, cache_pos, cache_live)
 
     keys_piece = lax.all_gather(new_keys, "ctx", axis=0, tiled=True)
-    values_piece = lax.all_gather(new_values, "ctx", axis=0, tiled=True)
+    values_piece = jnp.concatenate(
+        lax.all_to_all(jnp.stack([new_values] * lax.axis_size("ctx")), "ctx", 0, 0), axis=0
+    )
     piece_rows = keys_piece.shape[0]
     key_pos = length + lax.iota(jnp.int32, piece_rows)
     span_state = combine(

time: 326 us -> 303 us (0.929)
  blocking collectives: 66.1 us -> 32.8 us
  starting transfers between devices: 50.2 us -> 67.1 us
  waiting for transfers between devices: 82.5 us -> 73.5 us
    all_gather x1 -> x0, blocking collectives: 30.2 us -> none  [local(): values_piece = lax.all_gather(new_values, 'ctx', axis=0, tiled=True)]
    all_to_all x0 -> x1, starting transfers between devices: none -> 9.94 us  [local(): lax.all_to_all(jnp.stack([new_values] * lax.axis_size('ctx')), 'ctx', 0, 0)]
    ppermute x64, waiting for transfers between devices: 82.5 us -> 73.5 us  [from_behind(): lax.ppermute(x, axis, [(i, (i + by) % devices) for i in range(devices)])]
    ppermute x64, starting transfers between devices: 50.2 us -> 57.1 us  [from_behind(): lax.ppermute(x, axis, [(i, (i + by) % devices) for i in range(devices)])]
  transfers between devices with their start and end apart: 64 -> 65, of which waited for: 17 -> 16; matrix products, arithmetic and copies ran while one was open for 0% -> 31% of each run, Pallas kernels for 0% -> 0%
where the time goes in v1:
time: 303 us; the launch traced here: 300 us
  waiting for transfers between devices  73.5 us (24%)
  starting transfers between devices  67.1 us (22%)
  matrix products  53.6 us (18%)
  blocking collectives  32.8 us (11%)
  local copies, waits for them, and re-layouts  30.9 us (10%)
  other arithmetic  29.3 us (10%)
  loops' own time  12.3 us (4%)
    ppermute x64, waiting for transfers between devices, from_behind(): lax.ppermute(x, axis, [(i, (i + by) % devices) for i in range(devices)])  73.5 us
    ppermute x64, starting transfers between devices, from_behind(): lax.ppermute(x, axis, [(i, (i + by) % devices) for i in range(devices)])  57.1 us
    dot_general x17, matrix products, attend(): jnp.einsum('rkgd,nkd->rkgn', grouped, keys_grouped, preferred_element_typ...  40.8 us
    all_gather x1, blocking collectives, local(): keys_piece = lax.all_gather(new_keys, 'ctx', axis=0, tiled=True)  32.8 us
    while x80, local copies, waits for them, and re-layouts  19 us
    dot_general x17, matrix products, attend(): jnp.einsum('rkgn,nkd->rkgd', weights.astype(jnp.bfloat16), values_grouped...  12.8 us
    another operation x1, loops' own time, local(): lax.fori_loop(0, count, hop_one, (queries,) + empty_state(rows, heads))  12.3 us
    lt x16, other arithmetic, local(): cache_live = cache_pos < length  11.5 us
  transfers between devices with their start and end apart: 65, of which 16 were waited for; matrix products, arithmetic and copies ran while one was open for 31% of the time, Pallas kernels for 0%

profile of v1, /device:TPU:2, one launch (start us, length us, event | category | flops | bytes accessed | tf_op | source)
XLA Modules:
  0.0 300.1 jit_solution(971745505742986761)
XLA Ops:
  2.2 9.9 %all-to-all-start = ((bf16[16,4,512]{2,1,0:T(4,128)(2,1)}), bf16[16,4,512]{2,1,0:T(4,128)(2,1)S(1)}, u32[]{:S(2)}, u32[]{:S(2)}) async-start(bf16[16,4,512]{2,1,0:T(4,128)(2,1)} %stack.2), calls=%async_computation | async-start | bytes 131072 | tf_op jit(solution)/shard_map/all_to_all | solution.py:91
  13.7 32.8 %all-gather = bf16[16,4,512]{2,1,0:T(4,128)(2,1)S(1)} all-gather(bf16[1,4,512]{2,1,0:T(4,128)(2,1)} %bitcast.138), channel_id=1, replica_groups=mesh['req'=16,'ctx'=16] {'ctx'}, dimensions={0}, use_global_device_ids=true | all-gather | bytes 69632 | tf_op jit(solution)/shard_map/all_gather | solution.py:89
  47.2 4.1 %reshape.243 = bf16[2048,4,128]{2,1,0:T(4,128)(2,1)} reshape(bf16[2048,512]{1,0:T(8,128)(2,1)} %param.12) | data formatting | bytes 4194304 | tf_op jit(solution)/shard_map/while/body/eval_jaxpr/reshape | solution.py:22
  53.4 245.0 %while.24 = (s32[]{:T(128)}, bf16[4,8192]{1,0:T(4,128)(2,1)S(1)}, f32[4,8192]{1,0:T(4,128)S(1)}, f32[4,64]{1,0:T(4,128)S(1)}, f32[4,64]{1,0:T(4,128)S(1)}, /*ind...) while((s32[]{:T(128)}, bf16[4,8192]{1,0:T(4,128)(2,1)S(1)}, ...), condition=%wide.wide.region_4.5_spmd.clone.clone, body=%wide.wide.region_1.4_spmd.clone.clone.sunk | while | flops 273275904 | bytes 21383824 | solution.py:107
  55.0 2.5 fusion.68
  62.0 6.4 %collective-permute-done.2 = f32[4,64]{1,0:T(4,128)S(1)} collective-permute-done((f32[4,64]{1,0:T(4,128)S(1)}, f32[4,64]{1,0:T(4,128)S(1)}, u32[]{:S(2)}, u32[]{:S(2)}) %collective-permute-start.2) | collective-permute-done | bytes 1056 | tf_op jit(solution)/shard_map/while/body/eval_jaxpr/ppermute | solution.py:14
  70.1 2.5 fusion.68
  75.9 3.5 %collective-permute-start.3 = (f32[4,64]{1,0:T(4,128)S(1)}, f32[4,64]{1,0:T(4,128)S(1)}, u32[]{:S(2)}, u32[]{:S(2)}) collective-permute-start(f32[4,64]{1,0:T(4,128)S(1)} %get-tuple-element.509), channel_id=1, source_target_pairs={{0,1},{1,2},{2,3},{3,4},{4,5},{5,6},{6,7},{7,8},{8,9},{9,10},{10,1... | collective-permute-start | bytes 3080 | tf_op jit(solution)/shard_map/while/body/eval_jaxpr/ppermute | solution.py:14
  79.4 4.1 %collective-permute-done.2 = f32[4,64]{1,0:T(4,128)S(1)} collective-permute-done((f32[4,64]{1,0:T(4,128)S(1)}, f32[4,64]{1,0:T(4,128)S(1)}, u32[]{:S(2)}, u32[]{:S(2)}) %collective-permute-start.2) | collective-permute-done | bytes 1056 | tf_op jit(solution)/shard_map/while/body/eval_jaxpr/ppermute | solution.py:14
  85.1 2.5 fusion.68
  94.4 4.1 %collective-permute-done.2 = f32[4,64]{1,0:T(4,128)S(1)} collective-permute-done((f32[4,64]{1,0:T(4,128)S(1)}, f32[4,64]{1,0:T(4,128)S(1)}, u32[]{:S(2)}, u32[]{:S(2)}) %collective-permute-start.2) | collective-permute-done | bytes 1056 | tf_op jit(solution)/shard_map/while/body/eval_jaxpr/ppermute | solution.py:14
  100.1 2.5 fusion.68
  110.0 3.8 %collective-permute-done.2 = f32[4,64]{1,0:T(4,128)S(1)} collective-permute-done((f32[4,64]{1,0:T(4,128)S(1)}, f32[4,64]{1,0:T(4,128)S(1)}, u32[]{:S(2)}, u32[]{:S(2)}) %collective-permute-start.2) | collective-permute-done | bytes 1056 | tf_op jit(solution)/shard_map/while/body/eval_jaxpr/ppermute | solution.py:14
  122.6 3.0 collective-permute-start.3
  125.6 4.8 %collective-permute-done.2 = f32[4,64]{1,0:T(4,128)S(1)} collective-permute-done((f32[4,64]{1,0:T(4,128)S(1)}, f32[4,64]{1,0:T(4,128)S(1)}, u32[]{:S(2)}, u32[]{:S(2)}) %collective-permute-start.2) | collective-permute-done | bytes 1056 | tf_op jit(solution)/shard_map/while/body/eval_jaxpr/ppermute | solution.py:14
  137.8 3.7 %collective-permute-start.3 = (f32[4,64]{1,0:T(4,128)S(1)}, f32[4,64]{1,0:T(4,128)S(1)}, u32[]{:S(2)}, u32[]{:S(2)}) collective-permute-start(f32[4,64]{1,0:T(4,128)S(1)} %get-tuple-element.509), channel_id=1, source_target_pairs={{0,1},{1,2},{2,3},{3,4},{4,5},{5,6},{6,7},{7,8},{8,9},{9,10},{10,1... | collective-permute-start | bytes 3080 | tf_op jit(solution)/shard_map/while/body/eval_jaxpr/ppermute | solution.py:14
  141.4 5.6 %collective-permute-done.2 = f32[4,64]{1,0:T(4,128)S(1)} collective-permute-done((f32[4,64]{1,0:T(4,128)S(1)}, f32[4,64]{1,0:T(4,128)S(1)}, u32[]{:S(2)}, u32[]{:S(2)}) %collective-permute-start.2) | collective-permute-done | bytes 1056 | tf_op jit(solution)/shard_map/while/body/eval_jaxpr/ppermute | solution.py:14
  148.7 2.5 fusion.68
  156.4 6.5 %collective-permute-done.2 = f32[4,64]{1,0:T(4,128)S(1)} collective-permute-done((f32[4,64]{1,0:T(4,128)S(1)}, f32[4,64]{1,0:T(4,128)S(1)}, u32[]{:S(2)}, u32[]{:S(2)}) %collective-permute-start.2) | collective-permute-done | bytes 1056 | tf_op jit(solution)/shard_map/while/body/eval_jaxpr/ppermute | solution.py:14
  164.6 2.5 fusion.68
  170.4 2.7 collective-permute-start.3
  173.0 5.0 %collective-permute-done.2 = f32[4,64]{1,0:T(4,128)S(1)} collective-permute-done((f32[4,64]{1,0:T(4,128)S(1)}, f32[4,64]{1,0:T(4,128)S(1)}, u32[]{:S(2)}, u32[]{:S(2)}) %collective-permute-start.2) | collective-permute-done | bytes 1056 | tf_op jit(solution)/shard_map/while/body/eval_jaxpr/ppermute | solution.py:14
  179.6 2.5 fusion.68
  186.2 2.7 collective-permute-start.3
  188.9 4.1 %collective-permute-done.2 = f32[4,64]{1,0:T(4,128)S(1)} collective-permute-done((f32[4,64]{1,0:T(4,128)S(1)}, f32[4,64]{1,0:T(4,128)S(1)}, u32[]{:S(2)}, u32[]{:S(2)}) %collective-permute-start.2) | collective-permute-done | bytes 1056 | tf_op jit(solution)/shard_map/while/body/eval_jaxpr/ppermute | solution.py:14
  204.0 4.1 %collective-permute-done.2 = f32[4,64]{1,0:T(4,128)S(1)} collective-permute-done((f32[4,64]{1,0:T(4,128)S(1)}, f32[4,64]{1,0:T(4,128)S(1)}, u32[]{:S(2)}, u32[]{:S(2)}) %collective-permute-start.2) | collective-permute-done | bytes 1056 | tf_op jit(solution)/shard_map/while/body/eval_jaxpr/ppermute | solution.py:14
  219.0 4.1 %collective-permute-done.2 = f32[4,64]{1,0:T(4,128)S(1)} collective-permute-done((f32[4,64]{1,0:T(4,128)S(1)}, f32[4,64]{1,0:T(4,128)S(1)}, u32[]{:S(2)}, u32[]{:S(2)}) %collective-permute-start.2) | collective-permute-done | bytes 1056 | tf_op jit(solution)/shard_map/while/body/eval_jaxpr/ppermute | solution.py:14
  234.1 4.1 %collective-permute-done.2 = f32[4,64]{1,0:T(4,128)S(1)} collective-permute-done((f32[4,64]{1,0:T(4,128)S(1)}, f32[4,64]{1,0:T(4,128)S(1)}, u32[]{:S(2)}, u32[]{:S(2)}) %collective-permute-start.2) | collective-permute-done | bytes 1056 | tf_op jit(solution)/shard_map/while/body/eval_jaxpr/ppermute | solution.py:14
  249.1 4.1 %collective-permute-done.2 = f32[4,64]{1,0:T(4,128)S(1)} collective-permute-done((f32[4,64]{1,0:T(4,128)S(1)}, f32[4,64]{1,0:T(4,128)S(1)}, u32[]{:S(2)}, u32[]{:S(2)}) %collective-permute-start.2) | collective-permute-done | bytes 1056 | tf_op jit(solution)/shard_map/while/body/eval_jaxpr/ppermute | solution.py:14
  264.2 4.1 %collective-permute-done.2 = f32[4,64]{1,0:T(4,128)S(1)} collective-permute-done((f32[4,64]{1,0:T(4,128)S(1)}, f32[4,64]{1,0:T(4,128)S(1)}, u32[]{:S(2)}, u32[]{:S(2)}) %collective-permute-start.2) | collective-permute-done | bytes 1056 | tf_op jit(solution)/shard_map/while/body/eval_jaxpr/ppermute | solution.py:14
  279.2 4.1 %collective-permute-done.2 = f32[4,64]{1,0:T(4,128)S(1)} collective-permute-done((f32[4,64]{1,0:T(4,128)S(1)}, f32[4,64]{1,0:T(4,128)S(1)}, u32[]{:S(2)}, u32[]{:S(2)}) %collective-permute-start.2) | collective-permute-done | bytes 1056 | tf_op jit(solution)/shard_map/while/body/eval_jaxpr/ppermute | solution.py:14
  294.3 4.1 %collective-permute-done.2 = f32[4,64]{1,0:T(4,128)S(1)} collective-permute-done((f32[4,64]{1,0:T(4,128)S(1)}, f32[4,64]{1,0:T(4,128)S(1)}, u32[]{:S(2)}, u32[]{:S(2)}) %collective-permute-start.2) | collective-permute-done | bytes 1056 | tf_op jit(solution)/shard_map/while/body/eval_jaxpr/ppermute | solution.py:14
  (435 shorter events, 134.0 us)
Async XLA Ops:
  2.2 296.6 %all-to-all-start = ((bf16[16,4,512]{2,1,0:T(4,128)(2,1)}), bf16[16,4,512]{2,1,0:T(4,128)(2,1)S(1)}, u32[]{:S(2)}, u32[]{:S(2)}) async-start(bf16[16,4,512]{2,1,0:T(4,128)(2,1)} %stack.2), calls=%async_computation | async-start | bytes 131072 | tf_op jit(solution)/shard_map/all_to_all | solution.py:91
  60.5 7.9 %collective-permute-start.1 = (f32[4,8192]{1,0:T(4,128)S(1)}, f32[4,8192]{1,0:T(4,128)S(1)}, u32[]{:S(2)}, u32[]{:S(2)}) collective-permute-start(f32[4,8192]{1,0:T(4,128)S(1)} %fusion.71), channel_id=1, source_target_pairs={{0,1},{1,2},{2,3},{3,4},{4,5},{5,6},{6,7},{7,8},{8,9},{9,10},{10,1... | collective-permute-start | bytes 393224 | tf_op jit(solution)/shard_map/while/body/eval_jaxpr/ppermute | solution.py:14
  60.6 7.8 %collective-permute-start = (bf16[4,8192]{1,0:T(4,128)(2,1)S(1)}, bf16[4,8192]{1,0:T(4,128)(2,1)S(1)}, u32[]{:S(2)}, u32[]{:S(2)}) collective-permute-start(bf16[4,8192]{1,0:T(4,128)(2,1)S(1)} %copy.160), channel_id=1, source_target_pairs={{0,1},{1,2},{2,3},{3,4},{4,5},{5,6},{6,7},{7,8},{8,9},{9,10},{10,1... | collective-permute-start | bytes 196616 | tf_op jit(solution)/shard_map/while/body/eval_jaxpr/ppermute | solution.py:14
  75.6 7.9 %collective-permute-start.1 = (f32[4,8192]{1,0:T(4,128)S(1)}, f32[4,8192]{1,0:T(4,128)S(1)}, u32[]{:S(2)}, u32[]{:S(2)}) collective-permute-start(f32[4,8192]{1,0:T(4,128)S(1)} %fusion.71), channel_id=1, source_target_pairs={{0,1},{1,2},{2,3},{3,4},{4,5},{5,6},{6,7},{7,8},{8,9},{9,10},{10,1... | collective-permute-start | bytes 393224 | tf_op jit(solution)/shard_map/while/body/eval_jaxpr/ppermute | solution.py:14
  75.7 7.8 %collective-permute-start = (bf16[4,8192]{1,0:T(4,128)(2,1)S(1)}, bf16[4,8192]{1,0:T(4,128)(2,1)S(1)}, u32[]{:S(2)}, u32[]{:S(2)}) collective-permute-start(bf16[4,8192]{1,0:T(4,128)(2,1)S(1)} %copy.160), channel_id=1, source_target_pairs={{0,1},{1,2},{2,3},{3,4},{4,5},{5,6},{6,7},{7,8},{8,9},{9,10},{10,1... | collective-permute-start | bytes 196616 | tf_op jit(solution)/shard_map/while/body/eval_jaxpr/ppermute | solution.py:14
  90.6 7.9 %collective-permute-start.1 = (f32[4,8192]{1,0:T(4,128)S(1)}, f32[4,8192]{1,0:T(4,128)S(1)}, u32[]{:S(2)}, u32[]{:S(2)}) collective-permute-start(f32[4,8192]{1,0:T(4,128)S(1)} %fusion.71), channel_id=1, source_target_pairs={{0,1},{1,2},{2,3},{3,4},{4,5},{5,6},{6,7},{7,8},{8,9},{9,10},{10,1... | collective-permute-start | bytes 393224 | tf_op jit(solution)/shard_map/while/body/eval_jaxpr/ppermute | solution.py:14
  90.7 7.8 %collective-permute-start = (bf16[4,8192]{1,0:T(4,128)(2,1)S(1)}, bf16[4,8192]{1,0:T(4,128)(2,1)S(1)}, u32[]{:S(2)}, u32[]{:S(2)}) collective-permute-start(bf16[4,8192]{1,0:T(4,128)(2,1)S(1)} %copy.160), channel_id=1, source_target_pairs={{0,1},{1,2},{2,3},{3,4},{4,5},{5,6},{6,7},{7,8},{8,9},{9,10},{10,1... | collective-permute-start | bytes 196616 | tf_op jit(solution)/shard_map/while/body/eval_jaxpr/ppermute | solution.py:14
  105.7 8.2 %collective-permute-start.1 = (f32[4,8192]{1,0:T(4,128)S(1)}, f32[4,8192]{1,0:T(4,128)S(1)}, u32[]{:S(2)}, u32[]{:S(2)}) collective-permute-start(f32[4,8192]{1,0:T(4,128)S(1)} %fusion.71), channel_id=1, source_target_pairs={{0,1},{1,2},{2,3},{3,4},{4,5},{5,6},{6,7},{7,8},{8,9},{9,10},{10,1... | collective-permute-start | bytes 393224 | tf_op jit(solution)/shard_map/while/body/eval_jaxpr/ppermute | solution.py:14
  105.8 8.1 %collective-permute-start = (bf16[4,8192]{1,0:T(4,128)(2,1)S(1)}, bf16[4,8192]{1,0:T(4,128)(2,1)S(1)}, u32[]{:S(2)}, u32[]{:S(2)}) collective-permute-start(bf16[4,8192]{1,0:T(4,128)(2,1)S(1)} %copy.160), channel_id=1, source_target_pairs={{0,1},{1,2},{2,3},{3,4},{4,5},{5,6},{6,7},{7,8},{8,9},{9,10},{10,1... | collective-permute-start | bytes 196616 | tf_op jit(solution)/shard_map/while/body/eval_jaxpr/ppermute | solution.py:14
  121.0 9.4 %collective-permute-start.1 = (f32[4,8192]{1,0:T(4,128)S(1)}, f32[4,8192]{1,0:T(4,128)S(1)}, u32[]{:S(2)}, u32[]{:S(2)}) collective-permute-start(f32[4,8192]{1,0:T(4,128)S(1)} %fusion.71), channel_id=1, source_target_pairs={{0,1},{1,2},{2,3},{3,4},{4,5},{5,6},{6,7},{7,8},{8,9},{9,10},{10,1... | collective-permute-start | bytes 393224 | tf_op jit(solution)/shard_map/while/body/eval_jaxpr/ppermute | solution.py:14
  121.1 9.3 %collective-permute-start = (bf16[4,8192]{1,0:T(4,128)(2,1)S(1)}, bf16[4,8192]{1,0:T(4,128)(2,1)S(1)}, u32[]{:S(2)}, u32[]{:S(2)}) collective-permute-start(bf16[4,8192]{1,0:T(4,128)(2,1)S(1)} %copy.160), channel_id=1, source_target_pairs={{0,1},{1,2},{2,3},{3,4},{4,5},{5,6},{6,7},{7,8},{8,9},{9,10},{10,1... | collective-permute-start | bytes 196616 | tf_op jit(solution)/shard_map/while/body/eval_jaxpr/ppermute | solution.py:14
  122.5 7.8 %collective-permute-start.2 = (f32[4,64]{1,0:T(4,128)S(1)}, f32[4,64]{1,0:T(4,128)S(1)}, u32[]{:S(2)}, u32[]{:S(2)}) collective-permute-start(f32[4,64]{1,0:T(4,128)S(1)} %get-tuple-element.508), channel_id=1, source_target_pairs={{0,1},{1,2},{2,3},{3,4},{4,5},{5,6},{6,7},{7,8},{8,9},{9,10},{10,1... | collective-permute-start | bytes 3080 | tf_op jit(solution)/shard_map/while/body/eval_jaxpr/ppermute | solution.py:14
  137.5 9.6 %collective-permute-start.1 = (f32[4,8192]{1,0:T(4,128)S(1)}, f32[4,8192]{1,0:T(4,128)S(1)}, u32[]{:S(2)}, u32[]{:S(2)}) collective-permute-start(f32[4,8192]{1,0:T(4,128)S(1)} %fusion.71), channel_id=1, source_target_pairs={{0,1},{1,2},{2,3},{3,4},{4,5},{5,6},{6,7},{7,8},{8,9},{9,10},{10,1... | collective-permute-start | bytes 393224 | tf_op jit(solution)/shard_map/while/body/eval_jaxpr/ppermute | solution.py:14
  137.6 9.5 %collective-permute-start = (bf16[4,8192]{1,0:T(4,128)(2,1)S(1)}, bf16[4,8192]{1,0:T(4,128)(2,1)S(1)}, u32[]{:S(2)}, u32[]{:S(2)}) collective-permute-start(bf16[4,8192]{1,0:T(4,128)(2,1)S(1)} %copy.160), channel_id=1, source_target_pairs={{0,1},{1,2},{2,3},{3,4},{4,5},{5,6},{6,7},{7,8},{8,9},{9,10},{10,1... | collective-permute-start | bytes 196616 | tf_op jit(solution)/shard_map/while/body/eval_jaxpr/ppermute | solution.py:14
  137.7 9.4 %collective-permute-start.2 = (f32[4,64]{1,0:T(4,128)S(1)}, f32[4,64]{1,0:T(4,128)S(1)}, u32[]{:S(2)}, u32[]{:S(2)}) collective-permute-start(f32[4,64]{1,0:T(4,128)S(1)} %get-tuple-element.508), channel_id=1, source_target_pairs={{0,1},{1,2},{2,3},{3,4},{4,5},{5,6},{6,7},{7,8},{8,9},{9,10},{10,1... | collective-permute-start | bytes 3080 | tf_op jit(solution)/shard_map/while/body/eval_jaxpr/ppermute | solution.py:14
  137.8 9.3 %collective-permute-start.3 = (f32[4,64]{1,0:T(4,128)S(1)}, f32[4,64]{1,0:T(4,128)S(1)}, u32[]{:S(2)}, u32[]{:S(2)}) collective-permute-start(f32[4,64]{1,0:T(4,128)S(1)} %get-tuple-element.509), channel_id=1, source_target_pairs={{0,1},{1,2},{2,3},{3,4},{4,5},{5,6},{6,7},{7,8},{8,9},{9,10},{10,1... | collective-permute-start | bytes 3080 | tf_op jit(solution)/shard_map/while/body/eval_jaxpr/ppermute | solution.py:14
  154.3 8.7 %collective-permute-start.1 = (f32[4,8192]{1,0:T(4,128)S(1)}, f32[4,8192]{1,0:T(4,128)S(1)}, u32[]{:S(2)}, u32[]{:S(2)}) collective-permute-start(f32[4,8192]{1,0:T(4,128)S(1)} %fusion.71), channel_id=1, source_target_pairs={{0,1},{1,2},{2,3},{3,4},{4,5},{5,6},{6,7},{7,8},{8,9},{9,10},{10,1... | collective-permute-start | bytes 393224 | tf_op jit(solution)/shard_map/while/body/eval_jaxpr/ppermute | solution.py:14
  154.3 8.6 %collective-permute-start = (bf16[4,8192]{1,0:T(4,128)(2,1)S(1)}, bf16[4,8192]{1,0:T(4,128)(2,1)S(1)}, u32[]{:S(2)}, u32[]{:S(2)}) collective-permute-start(bf16[4,8192]{1,0:T(4,128)(2,1)S(1)} %copy.160), channel_id=1, source_target_pairs={{0,1},{1,2},{2,3},{3,4},{4,5},{5,6},{6,7},{7,8},{8,9},{9,10},{10,1... | collective-permute-start | bytes 196616 | tf_op jit(solution)/shard_map/while/body/eval_jaxpr/ppermute | solution.py:14
  154.4 8.5 %collective-permute-start.2 = (f32[4,64]{1,0:T(4,128)S(1)}, f32[4,64]{1,0:T(4,128)S(1)}, u32[]{:S(2)}, u32[]{:S(2)}) collective-permute-start(f32[4,64]{1,0:T(4,128)S(1)} %get-tuple-element.508), channel_id=1, source_target_pairs={{0,1},{1,2},{2,3},{3,4},{4,5},{5,6},{6,7},{7,8},{8,9},{9,10},{10,1... | collective-permute-start | bytes 3080 | tf_op jit(solution)/shard_map/while/body/eval_jaxpr/ppermute | solution.py:14
  154.5 8.4 %collective-permute-start.3 = (f32[4,64]{1,0:T(4,128)S(1)}, f32[4,64]{1,0:T(4,128)S(1)}, u32[]{:S(2)}, u32[]{:S(2)}) collective-permute-start(f32[4,64]{1,0:T(4,128)S(1)} %get-tuple-element.509), channel_id=1, source_target_pairs={{0,1},{1,2},{2,3},{3,4},{4,5},{5,6},{6,7},{7,8},{8,9},{9,10},{10,1... | collective-permute-start | bytes 3080 | tf_op jit(solution)/shard_map/while/body/eval_jaxpr/ppermute | solution.py:14
  170.1 7.9 %collective-permute-start.1 = (f32[4,8192]{1,0:T(4,128)S(1)}, f32[4,8192]{1,0:T(4,128)S(1)}, u32[]{:S(2)}, u32[]{:S(2)}) collective-permute-start(f32[4,8192]{1,0:T(4,128)S(1)} %fusion.71), channel_id=1, source_target_pairs={{0,1},{1,2},{2,3},{3,4},{4,5},{5,6},{6,7},{7,8},{8,9},{9,10},{10,1... | collective-permute-start | bytes 393224 | tf_op jit(solution)/shard_map/while/body/eval_jaxpr/ppermute | solution.py:14
  170.2 7.8 %collective-permute-start = (bf16[4,8192]{1,0:T(4,128)(2,1)S(1)}, bf16[4,8192]{1,0:T(4,128)(2,1)S(1)}, u32[]{:S(2)}, u32[]{:S(2)}) collective-permute-start(bf16[4,8192]{1,0:T(4,128)(2,1)S(1)} %copy.160), channel_id=1, source_target_pairs={{0,1},{1,2},{2,3},{3,4},{4,5},{5,6},{6,7},{7,8},{8,9},{9,10},{10,1... | collective-permute-start | bytes 196616 | tf_op jit(solution)/shard_map/while/body/eval_jaxpr/ppermute | solution.py:14
  185.2 7.9 %collective-permute-start.1 = (f32[4,8192]{1,0:T(4,128)S(1)}, f32[4,8192]{1,0:T(4,128)S(1)}, u32[]{:S(2)}, u32[]{:S(2)}) collective-permute-start(f32[4,8192]{1,0:T(4,128)S(1)} %fusion.71), channel_id=1, source_target_pairs={{0,1},{1,2},{2,3},{3,4},{4,5},{5,6},{6,7},{7,8},{8,9},{9,10},{10,1... | collective-permute-start | bytes 393224 | tf_op jit(solution)/shard_map/while/body/eval_jaxpr/ppermute | solution.py:14
  185.2 7.8 %collective-permute-start = (bf16[4,8192]{1,0:T(4,128)(2,1)S(1)}, bf16[4,8192]{1,0:T(4,128)(2,1)S(1)}, u32[]{:S(2)}, u32[]{:S(2)}) collective-permute-start(bf16[4,8192]{1,0:T(4,128)(2,1)S(1)} %copy.160), channel_id=1, source_target_pairs={{0,1},{1,2},{2,3},{3,4},{4,5},{5,6},{6,7},{7,8},{8,9},{9,10},{10,1... | collective-permute-start | bytes 196616 | tf_op jit(solution)/shard_map/while/body/eval_jaxpr/ppermute | solution.py:14
  200.2 7.9 %collective-permute-start.1 = (f32[4,8192]{1,0:T(4,128)S(1)}, f32[4,8192]{1,0:T(4,128)S(1)}, u32[]{:S(2)}, u32[]{:S(2)}) collective-permute-start(f32[4,8192]{1,0:T(4,128)S(1)} %fusion.71), channel_id=1, source_target_pairs={{0,1},{1,2},{2,3},{3,4},{4,5},{5,6},{6,7},{7,8},{8,9},{9,10},{10,1... | collective-permute-start | bytes 393224 | tf_op jit(solution)/shard_map/while/body/eval_jaxpr/ppermute | solution.py:14
  200.3 7.8 %collective-permute-start = (bf16[4,8192]{1,0:T(4,128)(2,1)S(1)}, bf16[4,8192]{1,0:T(4,128)(2,1)S(1)}, u32[]{:S(2)}, u32[]{:S(2)}) collective-permute-start(bf16[4,8192]{1,0:T(4,128)(2,1)S(1)} %copy.160), channel_id=1, source_target_pairs={{0,1},{1,2},{2,3},{3,4},{4,5},{5,6},{6,7},{7,8},{8,9},{9,10},{10,1... | collective-permute-start | bytes 196616 | tf_op jit(solution)/shard_map/while/body/eval_jaxpr/ppermute | solution.py:14
  215.2 7.9 %collective-permute-start.1 = (f32[4,8192]{1,0:T(4,128)S(1)}, f32[4,8192]{1,0:T(4,128)S(1)}, u32[]{:S(2)}, u32[]{:S(2)}) collective-permute-start(f32[4,8192]{1,0:T(4,128)S(1)} %fusion.71), channel_id=1, source_target_pairs={{0,1},{1,2},{2,3},{3,4},{4,5},{5,6},{6,7},{7,8},{8,9},{9,10},{10,1... | collective-permute-start | bytes 393224 | tf_op jit(solution)/shard_map/while/body/eval_jaxpr/ppermute | solution.py:14
  230.3 7.9 %collective-permute-start.1 = (f32[4,8192]{1,0:T(4,128)S(1)}, f32[4,8192]{1,0:T(4,128)S(1)}, u32[]{:S(2)}, u32[]{:S(2)}) collective-permute-start(f32[4,8192]{1,0:T(4,128)S(1)} %fusion.71), channel_id=1, source_target_pairs={{0,1},{1,2},{2,3},{3,4},{4,5},{5,6},{6,7},{7,8},{8,9},{9,10},{10,1... | collective-permute-start | bytes 393224 | tf_op jit(solution)/shard_map/while/body/eval_jaxpr/ppermute | solution.py:14
  245.3 7.9 %collective-permute-start.1 = (f32[4,8192]{1,0:T(4,128)S(1)}, f32[4,8192]{1,0:T(4,128)S(1)}, u32[]{:S(2)}, u32[]{:S(2)}) collective-permute-start(f32[4,8192]{1,0:T(4,128)S(1)} %fusion.71), channel_id=1, source_target_pairs={{0,1},{1,2},{2,3},{3,4},{4,5},{5,6},{6,7},{7,8},{8,9},{9,10},{10,1... | collective-permute-start | bytes 393224 | tf_op jit(solution)/shard_map/while/body/eval_jaxpr/ppermute | solution.py:14
  260.4 7.9 %collective-permute-start.1 = (f32[4,8192]{1,0:T(4,128)S(1)}, f32[4,8192]{1,0:T(4,128)S(1)}, u32[]{:S(2)}, u32[]{:S(2)}) collective-permute-start(f32[4,8192]{1,0:T(4,128)S(1)} %fusion.71), channel_id=1, source_target_pairs={{0,1},{1,2},{2,3},{3,4},{4,5},{5,6},{6,7},{7,8},{8,9},{9,10},{10,1... | collective-permute-start | bytes 393224 | tf_op jit(solution)/shard_map/while/body/eval_jaxpr/ppermute | solution.py:14
  275.4 7.9 %collective-permute-start.1 = (f32[4,8192]{1,0:T(4,128)S(1)}, f32[4,8192]{1,0:T(4,128)S(1)}, u32[]{:S(2)}, u32[]{:S(2)}) collective-permute-start(f32[4,8192]{1,0:T(4,128)S(1)} %fusion.71), channel_id=1, source_target_pairs={{0,1},{1,2},{2,3},{3,4},{4,5},{5,6},{6,7},{7,8},{8,9},{9,10},{10,1... | collective-permute-start | bytes 393224 | tf_op jit(solution)/shard_map/while/body/eval_jaxpr/ppermute | solution.py:14
  290.4 7.9 %collective-permute-start.1 = (f32[4,8192]{1,0:T(4,128)S(1)}, f32[4,8192]{1,0:T(4,128)S(1)}, u32[]{:S(2)}, u32[]{:S(2)}) collective-permute-start(f32[4,8192]{1,0:T(4,128)S(1)} %fusion.71), channel_id=1, source_target_pairs={{0,1},{1,2},{2,3},{3,4},{4,5},{5,6},{6,7},{7,8},{8,9},{9,10},{10,1... | collective-permute-start | bytes 393224 | tf_op jit(solution)/shard_map/while/body/eval_jaxpr/ppermute | solution.py:14
  (50 other events, 253.4 us)
